TPU v7x, 32 devices: a whole 2x2x4 slice. The times are simulated.
32 devices in a mesh: tm: 8 (over z, x), feat: 4 (over y, core).
Axes of the slice: x: 2, y: 2, z: 4, core: 2. Of those that a mesh axis runs over, the one named last changes fastest.
Arguments:
- coords: float32 [512, 3, 8, 256], P('tm'), may hold values from -12 to 12, as said below
- set_a: int32 [128], replicated, may hold values from 0 to 255
- set_b: int32 [128], replicated, may hold values from 0 to 255
Outputs:
- c00: float32 [16384, 16384], P('feat', 'tm')
- c0t: float32 [16384, 16384], P('feat', 'tm')
Inputs may be any that keep to these rules, and one draw needn't show every extreme that they name: `coords`: positions of a folding protein.
All inputs are finite; a program needn't handle non-finite values.
Results may differ from a plain program's by a relative error of at most 0.0003.
Values may be sent and summed in bfloat16 or wider, within the bound.
A program may use at most 128 MiB of HBM per device.

v0:
```python
import jax
import jax.numpy as jnp
from jax import lax
from jax.sharding import PartitionSpec as P

LAG = 64
contact_radius = 1.2
contact_width = 0.25


def contact_features(positions, index_a, index_b):
    part_a = jnp.take(positions, index_a, axis=3)
    part_b = jnp.take(positions, index_b, axis=3)
    frame_rows = positions.shape[0]
    summed = jnp.zeros((frame_rows, part_a.shape[3], part_b.shape[3]), jnp.float32)
    for first_atom in range(part_a.shape[2]):
        square = jnp.zeros(
            (frame_rows, part_b.shape[2], part_a.shape[3], part_b.shape[3]), jnp.float32
        )
        for component in range(3):
            difference = (
                part_a[:, component, first_atom, :][:, None, :, None]
                - part_b[:, component, :, :][:, :, None, :]
            )
            square = square + difference * difference
        summed = summed + jnp.sum(
            jax.nn.sigmoid((contact_radius - jnp.sqrt(square)) / contact_width), axis=1
        )
    summed = summed / float(part_a.shape[2])
    return summed.reshape(frame_rows, part_a.shape[3] * part_b.shape[3])


def contract_frames(left, right):
    return lax.dot_general(
        left, right, (((0,), (0,)), ((), ())), preferred_element_type=jnp.float32
    )


def pair_sums(frames_block, pairs):
    early = frames_block[:pairs].astype(jnp.float32)
    later = frames_block[LAG:].astype(jnp.float32)
    padding = jnp.zeros((LAG, frames_block.shape[1]), jnp.bfloat16)
    plus = jnp.concatenate([(early + later).astype(jnp.bfloat16), padding], axis=0)
    minus = jnp.concatenate([(early - later).astype(jnp.bfloat16), padding], axis=0)
    return (plus, minus)


def per_device(coords, set_a, set_b):
    feat_count = lax.axis_size("feat")
    feat_index = lax.axis_index("feat")
    rows_a = set_a.shape[0] // feat_count
    index_a = lax.dynamic_slice_in_dim(set_a, feat_index * rows_a, rows_a)
    lifted = contact_features(coords, index_a, set_b)
    frame_rows = coords.shape[0]
    time_count = lax.axis_size("tm")
    time_index = lax.axis_index("tm")
    frames_all = frame_rows * time_count
    pairs = frames_all - LAG
    frame_ids = time_index * frame_rows + jnp.arange(frame_rows, dtype=jnp.int32)
    weight = (frame_ids < pairs).astype(jnp.float32) + (frame_ids >= LAG).astype(jnp.float32)
    local_sums = jnp.dot(weight, lifted, precision=lax.Precision.HIGHEST)
    means = lax.psum(local_sums, "tm") / (2.0 * pairs)
    centered = (lifted - means[None, :]).astype(jnp.bfloat16)
    centered = lax.optimization_barrier(centered)
    every_feature = lax.all_gather(centered, "feat", axis=1, tiled=True)
    column_block = lax.all_to_all(every_feature, "tm", split_axis=1, concat_axis=0, tiled=True)
    plus_cols, minus_cols = pair_sums(column_block, pairs)
    gathered = lax.all_gather(centered, "tm", axis=0, tiled=True)
    plus_rows, minus_rows = pair_sums(gathered, pairs)
    sum_plus = contract_frames(plus_rows, plus_cols)
    sum_minus = contract_frames(minus_rows, minus_cols)
    c00 = (sum_plus + sum_minus) / (4.0 * pairs)
    c0t = (sum_plus - sum_minus) / (4.0 * pairs)
    return (c00, c0t)


def solution(mesh):
    placed = (P("tm", None, None, None), P(), P())
    return jax.shard_map(
        per_device,
        mesh=mesh,
        in_specs=placed,
        out_specs=(P("feat", "tm"), P("feat", "tm")),
        check_vma=False,
    )
```

profile of v0, /device:TPU:0, one launch (start us, length us, event | category | flops | bytes accessed | tf_op | source)
XLA Modules:
  0.0 303.0 jit_solution(4928474648640069345)
XLA Ops:
  7.2 0.0 all-gather.5.cloned.1.call-start
  7.2 0.7 compare_and_fusion
  7.9 0.7 compare_select_fusion
  8.5 0.7 compare_and_fusion.1
  9.3 2.3 copy.95
  11.6 0.6 gather_fusion
  12.2 0.1 select_bitcast_fusion.1
  12.3 0.1 fusion.35
  12.3 0.3 fusion.34
  12.7 1.9 gather_fusion.1
  14.6 1.6 select_bitcast_fusion
  16.2 0.1 slice_bitcast_fusion.2
  16.3 0.2 copy.98
  16.5 0.1 copy.104
  16.6 0.1 copy.103
  16.7 0.1 copy.123
  16.8 0.1 copy.115
  16.9 0.1 copy.101
  17.0 0.1 copy.99
  17.0 0.1 copy.96
  17.1 0.1 copy.122
  17.2 0.1 copy.121
  17.3 0.1 copy.120
  17.4 0.1 copy.119
  17.5 0.1 copy.118
  17.5 0.1 copy.117
  17.6 0.1 copy.116
  17.7 0.1 copy.114
  17.8 0.1 copy.113
  17.9 0.1 copy.112
  18.0 0.1 copy.111
  18.0 0.1 copy.110
  18.1 0.1 copy.109
  18.2 0.1 copy.108
  18.3 0.1 copy.107
  18.4 0.1 copy.106
  18.5 0.1 copy.105
  18.6 0.2 copy.102
  18.8 0.2 copy.100
  19.0 19.8 %fusion.7 = (f32[64,32,128]{2,1,0:T(8,128)S(1)}, f32[64,32,128]{2,1,0:T(8,128)S(1)}, f32[64,32,128]{2,1,0:T(8,128)S(1)}) fusion(f32[64,8,128]{2,1,0:T(8,128)S(1)} %copy.102, f32[64,32]{1,0:T(8,128)S(1)} %copy.101, f32[64,8,128]{2,1,0:T(8,128)S(1)} %copy.100, f32[64,32]{1,0:T(8,128)S(1)} %copy.99, f32[64,8,128]{2,1,0:T(8,128)S(1)} %copy.98, ...), kind=kLoop, calls=%fused_computation.21 | loop fusion | flops 87293952 | bytes 4005888 | tf_op jit(solution)/shard_map/reduce_sum | solution.py:26
  38.8 31.7 %fusion.6 = (f32[64,32,128]{2,1,0:T(8,128)S(1)}, f32[64,32,128]{2,1,0:T(8,128)S(1)}, f32[64,32,128]{2,1,0:T(8,128)S(1)}, f32[64,32,128]{2,1,0:T(8,128)S(1)}, f32[64,32,128]{2,1,0:T(8,128)S(1)}) fusion(f32[64,32]{1,0:T(8,128)S(1)} %copy.105, f32[64,32]{1,0:T(8,128)S(1)} %copy.104, f32[64,32]{1,0:T(8,128)S(1)} %copy.103, f32[64,8,128]{2,1,0:T(8,128)S(1)} %copy.102, ...), kind=kLoop, calls=%fused_computation.19 | loop fusion | flops 145489920 | bytes 6152192 | tf_op jit(solution)/shard_map/reduce_sum | solution.py:26
  70.5 1.0 add_multiply_fusion.1
  71.6 1.2 fusion.18
  72.7 38.8 %psum.7 = f32[4096]{0:T(1024)S(1)} all-reduce(f32[4096]{0:T(1024)S(1)} %bitcast.59), channel_id=1, replica_groups=mesh['tm'=8,'feat'=4] {'tm'}, use_global_device_ids=true, to_apply=%region_8.9 | all-reduce | flops 4096 | bytes 32768 | tf_op jit(solution)/shard_map/psum | solution.py:62
  111.6 1.4 fusion.20
  113.0 0.0 all-gather.5.cloned.1.call-update
  113.0 0.0 all-gather.3.cloned.1.call-start
  113.0 0.7 all-gather.3.cloned.1.call-update
  113.7 19.3 %all-gather.5.cloned.1.call-done = bf16[64,16384]{1,0:T(8,128)(2,1)} async-done(((bf16[64,4096]{1,0:T(8,128)(2,1)}), bf16[64,16384]{1,0:T(8,128)(2,1)}) %all-gather.5.cloned.1.call-update) | async-done | bytes 2097168 | tf_op jit(solution)/shard_map/all_gather | solution.py:65
  133.0 1.7 copy.133
  134.7 91.9 %all_to_all.16 = bf16[64,8,2048]{2,0,1:T(8,128)(2,1)S(1)} all-to-all(bf16[64,8,2048]{2,0,1:T(8,128)(2,1)S(1)} %bitcast.55), channel_id=1, replica_groups=mesh['tm'=8,'feat'=4] {'tm'}, dimensions={1} | all-to-all | bytes 4194304 | tf_op jit(solution)/shard_map/all_to_all | solution.py:66
  226.7 2.1 fusion.15
  228.8 11.0 %all-gather.3.cloned.1.call-done = bf16[512,4096]{1,0:T(8,128)(2,1)} async-done(((bf16[64,4096]{1,0:T(8,128)(2,1)}), bf16[512,4096]{1,0:T(8,128)(2,1)}) %all-gather.3.cloned.1.call-update) | async-done | bytes 4194320 | tf_op jit(solution)/shard_map/all_gather | solution.py:68
  239.7 0.0 copy-start
  239.7 5.5 %fusion.9 = (bf16[448,4096]{1,0:T(8,128)(2,1)S(1)}, bf16[448,4096]{1,0:T(8,128)(2,1)}) fusion(bf16[512,4096]{1,0:T(8,128)(2,1)} %all-gather.3.cloned.1.call-done), kind=kLoop, calls=%fused_computation.23 | loop fusion | flops 11010048 | bytes 14680064 | tf_op jit(solution)/shard_map/convert_element_type | solution.py:44
  245.2 0.0 copy-done
  245.2 16.3 %fusion.10 = f32[4096,2048]{1,0:T(8,128)} fusion(bf16[448,4096]{1,0:T(8,128)(2,1)S(1)} %get-tuple-element.14, bf16[448,2048]{1,0:T(8,128)(2,1)S(1)} %bitcast.58), kind=kOutput, calls=%fused_computation.26 | convolution fusion | flops 8589934592 | bytes 39059456 | tf_op jit(solution)/shard_map/dot_general | solution.py:34
  261.5 34.7 %subtract_multiply_fusion = (f32[4096,2048]{1,0:T(8,128)}, f32[4096,2048]{1,0:T(8,128)}) fusion(f32[4096,2048]{1,0:T(8,128)} %fusion.10, bf16[448,2048]{1,0:T(8,128)(2,1)S(1)} %bitcast.56, bf16[448,4096]{1,0:T(8,128)(2,1)} %get-tuple-element.15), kind=kOutput, calls=%fused_computation.2 | convolution fusion | flops 8623489024 | bytes 106168320 | tf_op jit(solution)/shard_map/dot_general | solution.py:34
  (3 shorter events, 0.0 us)
Async XLA Ops:
  7.2 125.8 %all-gather.5.cloned.1.call-start = ((), (), s32[]{:S(2)}) async-start(), calls=%async_computation.2 | async-start | bytes 2621440 | tf_op jit(solution)/shard_map/all_gather | solution.py:65
  113.0 126.7 %all-gather.3.cloned.1.call-start = ((), (), s32[]{:S(2)}) async-start(), calls=%async_computation.1 | async-start | bytes 4718592 | tf_op jit(solution)/shard_map/all_gather | solution.py:68
  239.7 5.5 %copy-start = (bf16[7,64,2048]{2,1,0:T(8,128)(2,1)S(1)}, bf16[7,64,2048]{2,1,0:T(8,128)(2,1)}, u32[]{:S(2)}) copy-start(bf16[7,64,2048]{2,1,0:T(8,128)(2,1)} %get-tuple-element.16) | copy-start | bytes 5505028
Sparse Core Ops, SparseCore 0:
  113.1 19.8 all-gather.4
  135.7 103.9 all-gather.2
where the time goes:
time: 303 us
  blocking collectives  131 us (43%)
  other arithmetic  65.3 us (22%)
  matrix products  52.1 us (17%)
  waiting for transfers between devices  30.9 us (10%)
  between operations  14.2 us (5%)
  local copies, waits for them, and re-layouts  9.68 us (3%)
    all_to_all x1, blocking collectives, per_device(): lax.all_to_all(every_feature, 'tm', split_axis=1, concat_axis=0, tiled=True)  91.9 us
    reduce_sum x2, other arithmetic, contact_features(): jnp.sum(jax.nn.sigmoid((contact_radius - jnp.sqrt(square)) / contact_widt...  51.5 us
    dot_general x2, matrix products, contract_frames(): lax.dot_general(left, right, (((0,), (0,)), ((), ())), preferred_element_...  50.9 us
    psum x1, blocking collectives, per_device(): means = lax.psum(local_sums, 'tm') / (2.0 * pairs)  38.8 us
    all_gather x1, waiting for transfers between devices, per_device(): every_feature = lax.all_gather(centered, 'feat', axis=1, tiled=True)  19.3 us
    all_gather x1, waiting for transfers between devices, per_device(): gathered = lax.all_gather(centered, 'tm', axis=0, tiled=True)  11 us
    convert_element_type x2, other arithmetic, pair_sums(): (early - later).astype(jnp.bfloat16)  7.62 us
  transfers between devices with their start and end apart: 2, of which 2 were waited for; matrix products, arithmetic and copies ran while one was open for 1% of the time, Pallas kernels for 0%

commit v1 on v0

--- a/solution.py
+++ b/solution.py
@@ -62,7 +62,7 @@
     means = lax.psum(local_sums, "tm") / (2.0 * pairs)
     centered = (lifted - means[None, :]).astype(jnp.bfloat16)
     centered = lax.optimization_barrier(centered)
-    every_feature = lax.all_gather(centered, "feat", axis=1, tiled=True)
+    every_feature = jnp.concatenate(lax.all_gather(centered, "feat"), axis=1)
     column_block = lax.all_to_all(every_feature, "tm", split_axis=1, concat_axis=0, tiled=True)
     plus_cols, minus_cols = pair_sums(column_block, pairs)
     gathered = lax.all_gather(centered, "tm", axis=0, tiled=True)

time: 303 us -> 308 us (1.017)
  waiting for transfers between devices: 30.9 us -> 23.8 us
  local copies, waits for them, and re-layouts: 9.68 us -> 15.9 us
  blocking collectives: 131 us -> 136 us
    all_gather x1, waiting for transfers between devices: 11 us -> 3.97 us  [per_device(): gathered = lax.all_gather(centered, 'tm', axis=0, tiled=True)]
    all_to_all x1, blocking collectives: 91.9 us -> 96.9 us  [per_device(): lax.all_to_all(every_feature, 'tm', split_axis=1, concat_axis=0, tiled=True)]
    reshape x0 -> x1, local copies, waits for them, and re-layouts: none -> 3.21 us  [per_device(): every_feature = jnp.concatenate(lax.all_gather(centered, 'feat'), axis=1)]
  transfers between devices with their start and end apart: 2 -> 2, of which waited for: 2 -> 2; matrix products, arithmetic and copies ran while one was open for 1% -> 3% of each run, Pallas kernels for 0% -> 0%
where the time goes in v1:
time: 308 us; the launch traced here: 307 us
  blocking collectives  136 us (44%)
  other arithmetic  65.3 us (21%)
  matrix products  52.1 us (17%)
  waiting for transfers between devices  23.8 us (8%)
  local copies, waits for them, and re-layouts  15.9 us (5%)
  between operations  14.2 us (5%)
    all_to_all x1, blocking collectives, per_device(): lax.all_to_all(every_feature, 'tm', split_axis=1, concat_axis=0, tiled=True)  96.9 us
    reduce_sum x2, other arithmetic, contact_features(): jnp.sum(jax.nn.sigmoid((contact_radius - jnp.sqrt(square)) / contact_widt...  51.5 us
    dot_general x2, matrix products, contract_frames(): lax.dot_general(left, right, (((0,), (0,)), ((), ())), preferred_element_...  50.9 us
    psum x1, blocking collectives, per_device(): means = lax.psum(local_sums, 'tm') / (2.0 * pairs)  38.8 us
    all_gather x1, waiting for transfers between devices, per_device(): every_feature = jnp.concatenate(lax.all_gather(centered, 'feat'), axis=1)  19.3 us
    convert_element_type x2, other arithmetic, pair_sums(): (early - later).astype(jnp.bfloat16)  7.62 us
  transfers between devices with their start and end apart: 2, of which 2 were waited for; matrix products, arithmetic and copies ran while one was open for 3% of the time, Pallas kernels for 0%

profile of v1, /device:TPU:0, one launch (start us, length us, event | category | flops | bytes accessed | tf_op | source)
XLA Modules:
  0.0 307.2 jit_solution(10904711291934244810)
XLA Ops:
  7.2 0.0 all-gather.6.cloned.1.call-start
  7.2 0.7 compare_and_fusion
  7.9 0.7 compare_select_fusion
  8.5 0.7 compare_and_fusion.1
  9.3 2.3 copy.99
  11.6 0.6 gather_fusion
  12.2 0.1 select_bitcast_fusion.1
  12.3 0.1 fusion.35
  12.3 0.3 fusion.34
  12.7 1.9 gather_fusion.1
  14.6 1.6 select_bitcast_fusion
  16.2 0.1 slice_bitcast_fusion.2
  16.3 0.2 copy.102
  16.5 0.1 copy.108
  16.6 0.1 copy.107
  16.7 0.1 copy.127
  16.8 0.1 copy.119
  16.9 0.1 copy.105
  17.0 0.1 copy.103
  17.0 0.1 copy.100
  17.1 0.1 copy.126
  17.2 0.1 copy.125
  17.3 0.1 copy.124
  17.4 0.1 copy.123
  17.5 0.1 copy.122
  17.5 0.1 copy.121
  17.6 0.1 copy.120
  17.7 0.1 copy.118
  17.8 0.1 copy.117
  17.9 0.1 copy.116
  18.0 0.1 copy.115
  18.0 0.1 copy.114
  18.1 0.1 copy.113
  18.2 0.1 copy.112
  18.3 0.1 copy.111
  18.4 0.1 copy.110
  18.5 0.1 copy.109
  18.6 0.2 copy.106
  18.8 0.2 copy.104
  19.0 19.8 %fusion.7 = (f32[64,32,128]{2,1,0:T(8,128)S(1)}, f32[64,32,128]{2,1,0:T(8,128)S(1)}, f32[64,32,128]{2,1,0:T(8,128)S(1)}) fusion(f32[64,8,128]{2,1,0:T(8,128)S(1)} %copy.106, f32[64,32]{1,0:T(8,128)S(1)} %copy.105, f32[64,8,128]{2,1,0:T(8,128)S(1)} %copy.104, f32[64,32]{1,0:T(8,128)S(1)} %copy.103, f32[64,8,128]{2,1,0:T(8,128)S(1)} %copy.102, ...), kind=kLoop, calls=%fused_computation.21 | loop fusion | flops 87293952 | bytes 4005888 | tf_op jit(solution)/shard_map/reduce_sum | solution.py:26
  38.8 31.7 %fusion.6 = (f32[64,32,128]{2,1,0:T(8,128)S(1)}, f32[64,32,128]{2,1,0:T(8,128)S(1)}, f32[64,32,128]{2,1,0:T(8,128)S(1)}, f32[64,32,128]{2,1,0:T(8,128)S(1)}, f32[64,32,128]{2,1,0:T(8,128)S(1)}) fusion(f32[64,32]{1,0:T(8,128)S(1)} %copy.109, f32[64,32]{1,0:T(8,128)S(1)} %copy.108, f32[64,32]{1,0:T(8,128)S(1)} %copy.107, f32[64,8,128]{2,1,0:T(8,128)S(1)} %copy.106, ...), kind=kLoop, calls=%fused_computation.19 | loop fusion | flops 145489920 | bytes 6152192 | tf_op jit(solution)/shard_map/reduce_sum | solution.py:26
  70.5 1.0 add_multiply_fusion.1
  71.6 1.2 fusion.18
  72.7 38.8 %psum.7 = f32[4096]{0:T(1024)S(1)} all-reduce(f32[4096]{0:T(1024)S(1)} %bitcast.57), channel_id=1, replica_groups=mesh['tm'=8,'feat'=4] {'tm'}, use_global_device_ids=true, to_apply=%region_8.9 | all-reduce | flops 4096 | bytes 32768 | tf_op jit(solution)/shard_map/psum | solution.py:62
  111.6 1.4 fusion.20
  113.0 0.0 all-gather.6.cloned.1.call-update
  113.0 0.2 all-gather.4.cloned.1.call-start
  113.2 0.5 all-gather.4.cloned.1.call-update
  113.7 19.3 %all-gather.6.cloned.1.call-done = bf16[256,4096]{1,0:T(8,128)(2,1)} async-done(((bf16[64,4096]{1,0:T(8,128)(2,1)}), bf16[256,4096]{1,0:T(8,128)(2,1)}) %all-gather.6.cloned.1.call-update) | async-done | bytes 2097168 | tf_op jit(solution)/shard_map/all_gather | solution.py:65
  133.0 3.2 %copy.128 = bf16[64,4,4096]{2,1,0:T(4,128)(2,1)S(1)} copy(bf16[64,4,4096]{2,0,1:T(8,128)(2,1)} %bitcast.55) | data formatting | bytes 4194304 | tf_op jit(solution)/shard_map/reshape | solution.py:65
  136.2 2.0 all_to_all.12
  138.2 2.7 copy.129
  141.0 96.9 %all_to_all.16 = bf16[64,8,2048]{2,0,1:T(8,128)(2,1)S(1)} all-to-all(bf16[64,8,2048]{2,0,1:T(8,128)(2,1)S(1)} %copy.129), channel_id=1, replica_groups=mesh['tm'=8,'feat'=4] {'tm'}, dimensions={1} | all-to-all | bytes 4194304 | tf_op jit(solution)/shard_map/all_to_all | solution.py:66
  237.8 2.1 fusion.15
  239.9 4.0 %all-gather.4.cloned.1.call-done = bf16[512,4096]{1,0:T(8,128)(2,1)} async-done(((bf16[64,4096]{1,0:T(8,128)(2,1)}), bf16[512,4096]{1,0:T(8,128)(2,1)}) %all-gather.4.cloned.1.call-update) | async-done | bytes 4194320 | tf_op jit(solution)/shard_map/all_gather | solution.py:68
  243.9 0.0 copy-start
  243.9 5.5 %fusion.9 = (bf16[448,4096]{1,0:T(8,128)(2,1)S(1)}, bf16[448,4096]{1,0:T(8,128)(2,1)}) fusion(bf16[512,4096]{1,0:T(8,128)(2,1)} %all-gather.4.cloned.1.call-done), kind=kLoop, calls=%fused_computation.23 | loop fusion | flops 11010048 | bytes 14680064 | tf_op jit(solution)/shard_map/convert_element_type | solution.py:44
  249.4 0.0 copy-done
  249.4 16.3 %fusion.10 = f32[4096,2048]{1,0:T(8,128)} fusion(bf16[448,4096]{1,0:T(8,128)(2,1)S(1)} %get-tuple-element.14, bf16[448,2048]{1,0:T(8,128)(2,1)S(1)} %bitcast.56), kind=kOutput, calls=%fused_computation.26 | convolution fusion | flops 8589934592 | bytes 39059456 | tf_op jit(solution)/shard_map/dot_general | solution.py:34
  265.7 34.7 %subtract_multiply_fusion = (f32[4096,2048]{1,0:T(8,128)}, f32[4096,2048]{1,0:T(8,128)}) fusion(f32[4096,2048]{1,0:T(8,128)} %fusion.10, bf16[448,2048]{1,0:T(8,128)(2,1)S(1)} %bitcast.54, bf16[448,4096]{1,0:T(8,128)(2,1)} %get-tuple-element.15), kind=kOutput, calls=%fused_computation.2 | convolution fusion | flops 8623489024 | bytes 106168320 | tf_op jit(solution)/shard_map/dot_general | solution.py:34
  (3 shorter events, 0.0 us)
Async XLA Ops:
  7.2 125.8 %all-gather.6.cloned.1.call-start = ((), (), s32[]{:S(2)}) async-start(), calls=%async_computation.2 | async-start | bytes 2621440 | tf_op jit(solution)/shard_map/all_gather | solution.py:65
  113.0 130.9 %all-gather.4.cloned.1.call-start = ((), (), s32[]{:S(2)}) async-start(), calls=%async_computation.1 | async-start | bytes 4718592 | tf_op jit(solution)/shard_map/all_gather | solution.py:68
  243.9 5.5 %copy-start = (bf16[7,64,2048]{2,1,0:T(8,128)(2,1)S(1)}, bf16[7,64,2048]{2,1,0:T(8,128)(2,1)}, u32[]{:S(2)}) copy-start(bf16[7,64,2048]{2,1,0:T(8,128)(2,1)} %get-tuple-element.16) | copy-start | bytes 5505028
Sparse Core Ops, SparseCore 0:
  113.1 19.8 all-gather.5
  135.7 108.1 all-gather.3
